TPU v7x, 256 devices: a whole 4x4x8 slice. The times are simulated.
256 devices in a mesh: gx: 16 (over z, core), gy: 16 (over x, y).
Axes of the slice: x: 4, y: 4, z: 8, core: 2. Of those that a mesh axis runs over, the one named last changes fastest.
Arguments:
- ref_pos: float32 [3, 131072], P(None, ('gx', 'gy')), as said below
- disp: float32 [3, 131072], P(None, ('gx', 'gy')), may hold values from -0.18 to 0.18
- volume: float32 [131072], P(('gx', 'gy')), may hold values from 0.6 to 1.4
- plastic: float32 [6, 131072], P(None, ('gx', 'gy')), may hold values from -0.06 to 0.06
- material: int32 [131072], P(('gx', 'gy')), may hold values from 0 to 2
- pair_list: int32 [256, 3, 26], P(('gx', 'gy')), may hold values from 0 to 8, as said below
- pair_count: int32 [256], P(('gx', 'gy')), may hold values from 6 to 22, as said below
Outputs:
- force: float32 [3, 131072], P(None, ('gx', 'gy'))
- plastic_new: float32 [6, 131072], P(None, ('gx', 'gy'))
Inputs may be any that keep to these rules, and one draw needn't show every extreme that they name: `pair_list`: entries 0 to pair_count - 1 of a device's list name distinct pairs of blocks that touch in the plane (a king's move in the grid of blocks), its own block first; every such pair of different blocks appears in exactly one device's list, in the list of one of its two owners; every device lists some pair with each of the devices beside it along gx and along gy; entries from pair_count on are 0, 0, 4. Direction 4 is the device itself, and no entry names a device off the grid. `pair_count`: some device holds 22 live entries in every draw. `ref_pos`: particles sit within 0.3 of a lattice of unit spacing, 4 x 4 x 8 to a block, blocks of a device in a 2 x 2 grid, devices in the gx, gy grid.
All inputs are finite; a program needn't handle non-finite values.
Results may differ from a plain program's by a relative error of at most 0.00019.
Values sent between devices are 32-bit elements; how exact they have to be, the bound alone decides.
A program may use at most 64 MiB of HBM per device.

v0:
```python
import jax
import jax.numpy as jnp
from jax import lax
from jax.sharding import PartitionSpec as P

BLOCK = 128


RADIUS = 2.0
KERNEL_SCALE = 1.5
REGULAR_SHIFT = 0.1
SHEAR_TABLE = (30.0, 40.0, 60.0)
BULK_TABLE = (60.0, 80.0, 120.0)
YIELD_TABLE = (1.0, 1.4, 2.2)
SYM_PAIRS = ((0, 0), (1, 1), (2, 2), (0, 1), (0, 2), (1, 2))


def passed_along(block, axis, distance):
    devices = range(lax.axis_size(axis))
    route = [(i - distance, i) for i in devices if i - distance in devices]
    return lax.ppermute(block, axis, route)


def with_halo(array, sides, width):
    for axis, dim in sides:
        devices, length = (lax.axis_size(axis), array.shape[dim])
        up = [(i, (i + 1) % devices) for i in range(devices - 1)]
        down = [(j, i) for i, j in up]
        last = lax.slice_in_dim(array, length - width, length, axis=dim)
        leading = lax.slice_in_dim(array, 0, width, axis=dim)
        before = lax.ppermute(last, axis, up)
        after = lax.ppermute(leading, axis, down)
        array = jnp.concatenate([before, array, after], axis=dim)
    return array


def kernel_parts(left, right):
    offset = right[0:3, None, :] - left[0:3, :, None]
    dist = jnp.sqrt(jnp.sum(offset * offset, axis=0))
    weight = KERNEL_SCALE * jnp.maximum(1.0 - dist / RADIUS, 0.0) ** 3
    return (offset, weight)


def moment_tile(left, right):
    offset, weight = kernel_parts(left, right)
    moved = offset + (right[3:6, None, :] - left[3:6, :, None])
    terms = [weight * offset[row_axis] * offset[col_axis] for row_axis, col_axis in SYM_PAIRS]
    terms = terms + [
        weight * moved[row_axis] * offset[col_axis]
        for row_axis in range(3)
        for col_axis in range(3)
    ]
    terms = jnp.stack(terms)
    home = jnp.sum(terms * right[6][None, None, :], axis=2)
    far = jnp.sum(terms * left[6][None, :, None], axis=1)
    return (home, far)


def force_tile(left, right):
    offset, weight = kernel_parts(left, right)
    scaled = weight * left[6][:, None] * right[6][None, :]
    comps = []
    for row_axis in range(3):
        inner = 0.0
        for col_axis in range(3):
            entry = 7 + 3 * row_axis + col_axis
            inner = inner + (left[entry][:, None] + right[entry][None, :]) * offset[col_axis]
        comps.append(scaled * inner)
    terms = jnp.stack(comps)
    return (jnp.sum(terms, axis=2), -jnp.sum(terms, axis=1))


def constitutive(moments, plastic, material):
    m00 = moments[0] + REGULAR_SHIFT
    m11 = moments[1] + REGULAR_SHIFT
    m22 = moments[2] + REGULAR_SHIFT
    m01, m02, m12 = (moments[3], moments[4], moments[5])
    c00 = m11 * m22 - m12 * m12
    c01 = m02 * m12 - m01 * m22
    c02 = m01 * m12 - m02 * m11
    c11 = m00 * m22 - m02 * m02
    c12 = m01 * m02 - m00 * m12
    c22 = m00 * m11 - m01 * m01
    determ = m00 * c00 + m01 * c01 + m02 * c02
    correct = [
        [c00 / determ, c01 / determ, c02 / determ],
        [c01 / determ, c11 / determ, c12 / determ],
        [c02 / determ, c12 / determ, c22 / determ],
    ]
    stretch = [
        [
            moments[6 + 3 * row_axis + col_axis] + (REGULAR_SHIFT if row_axis == col_axis else 0.0)
            for col_axis in range(3)
        ]
        for row_axis in range(3)
    ]
    grad = [
        [
            stretch[row_axis][0] * correct[0][col_axis]
            + stretch[row_axis][1] * correct[1][col_axis]
            + stretch[row_axis][2] * correct[2][col_axis]
            for col_axis in range(3)
        ]
        for row_axis in range(3)
    ]
    strain = []
    for index_sym, (row_axis, col_axis) in enumerate(SYM_PAIRS):
        value = 0.5 * (grad[row_axis][col_axis] + grad[col_axis][row_axis]) - plastic[index_sym]
        if row_axis == col_axis:
            value = value - 1.0
        strain.append(value)
    selector = (material[None, :] == jnp.arange(3, dtype=jnp.int32)[:, None]).astype(jnp.float32)
    shear = jnp.sum(jnp.asarray(SHEAR_TABLE, jnp.float32)[:, None] * selector, axis=0)
    bulk = jnp.sum(jnp.asarray(BULK_TABLE, jnp.float32)[:, None] * selector, axis=0)
    yield_stress = jnp.sum(jnp.asarray(YIELD_TABLE, jnp.float32)[:, None] * selector, axis=0)
    trace_part = strain[0] + strain[1] + strain[2]
    deviator = [
        strain[index_sym] - (trace_part / 3.0 if index_sym < 3 else 0.0) for index_sym in range(6)
    ]
    trial = [2.0 * shear * value for value in deviator]
    squares = (
        trial[0] ** 2
        + trial[1] ** 2
        + trial[2] ** 2
        + 2.0 * (trial[3] ** 2 + trial[4] ** 2 + trial[5] ** 2)
    )
    equiv = jnp.sqrt(1.5 * squares)
    factor = yield_stress / jnp.maximum(equiv, yield_stress)
    plastic_new = jnp.stack(
        [plastic[index_sym] + (1.0 - factor) * deviator[index_sym] for index_sym in range(6)]
    )
    sym_stress = [
        factor * trial[index_sym] + (bulk * trace_part if index_sym < 3 else 0.0)
        for index_sym in range(6)
    ]
    full = [
        [sym_stress[0], sym_stress[3], sym_stress[4]],
        [sym_stress[3], sym_stress[1], sym_stress[5]],
        [sym_stress[4], sym_stress[5], sym_stress[2]],
    ]
    piola = jnp.stack(
        [
            full[row_axis][0] * correct[0][col_axis]
            + full[row_axis][1] * correct[1][col_axis]
            + full[row_axis][2] * correct[2][col_axis]
            for row_axis in range(3)
            for col_axis in range(3)
        ]
    )
    return (piola, plastic_new)


def self_sums(nearby, tile_fn, home_acc):
    nblocks = nearby.shape[2]

    def self_visit(block_index, accum):
        tile = nearby[4][:, block_index]
        return accum.at[:, block_index].add(tile_fn(tile, tile)[0])

    return lax.fori_loop(0, nblocks, self_visit, home_acc)


def listed_sums(nearby, lists, total, tile_fn, width):
    nblocks = nearby.shape[2]
    home_acc = jnp.zeros((width, nblocks, BLOCK), jnp.float32)
    far_acc = jnp.zeros((9, width, nblocks, BLOCK), jnp.float32)

    def listed_visit(slot, carry):
        home_part, far_part = carry
        first = lists[0, slot]
        second = lists[1, slot]
        where_dir = lists[2, slot]
        home, far = tile_fn(nearby[4][:, first], nearby[where_dir][:, second])
        home_part = home_part.at[:, first].add(home)
        far_part = far_part.at[where_dir, :, second].add(far)
        return (home_part, far_part)

    home_acc, far_acc = lax.fori_loop(0, total, listed_visit, (home_acc, far_acc))
    home_acc = self_sums(nearby, tile_fn, home_acc)
    return (home_acc.reshape(width, nblocks * BLOCK), far_acc.reshape(3, 3, width, nblocks * BLOCK))


def fold_sectioned(home_part, far_grid, shift_width, shift_length):
    column = far_grid[1] + shift_width(far_grid[2], 1) + shift_width(far_grid[0], -1)
    return home_part + column[1] + shift_length(column[2], 1) + shift_length(column[0], -1)


def moment_width(piece, offset_sign):
    return passed_along(piece, "gx", offset_sign)


def moment_length(piece, offset_sign):
    return passed_along(piece, "gy", offset_sign)


def force_width(piece, offset_sign):
    return passed_along(piece, "gx", offset_sign)


def force_length(piece, offset_sign):
    return passed_along(piece, "gy", offset_sign)


def on_device(ref_pos, disp, volume, plastic, material, pair_list, pair_count):
    count_slots = ref_pos.shape[1]
    nblocks = count_slots // BLOCK
    state = jnp.concatenate([ref_pos, disp, volume[None, :]], axis=0)
    nearby = with_halo(state.reshape(1, 1, 7, count_slots), (("gx", 0), ("gy", 1)), 1)
    nearby = nearby.reshape(9, 7, nblocks, BLOCK)
    lists = pair_list[0]
    total = pair_count[0]
    home_part, far_part = listed_sums(nearby, lists, total, moment_tile, 15)
    moments = fold_sectioned(home_part, far_part, moment_width, moment_length)
    piola, plastic_new = constitutive(moments, plastic, material)
    near_stress = with_halo(piola.reshape(1, 1, 9, count_slots), (("gx", 0), ("gy", 1)), 1)
    nearby_two = jnp.concatenate([nearby, near_stress.reshape(9, 9, nblocks, BLOCK)], axis=1)
    home_force, far_force = listed_sums(nearby_two, lists, total, force_tile, 3)
    force = fold_sectioned(home_force, far_force, force_width, force_length)
    return (force, plastic_new)


def solution(mesh):
    in_specs = (
        P(None, ("gx", "gy")),
        P(None, ("gx", "gy")),
        P(("gx", "gy")),
        P(None, ("gx", "gy")),
        P(("gx", "gy")),
        P(("gx", "gy"), None, None),
        P(("gx", "gy")),
    )
    out_specs = (P(None, ("gx", "gy")), P(None, ("gx", "gy")))
    return jax.shard_map(
        on_device, mesh=mesh, in_specs=in_specs, out_specs=out_specs, check_vma=False
    )
```

profile of v0, /device:TPU:17, one launch (start us, length us, event | category | flops | bytes accessed | tf_op | source)
XLA Modules:
  0.0 565.5 jit_solution(11727248367804230157)
XLA Ops:
  1.4 4.2 collective-permute-start
  5.7 1.9 collective-permute-start.1
  7.6 3.1 collective-permute-done.1
  10.7 2.9 collective-permute-start.2
  13.7 2.4 collective-permute-start.3
  16.2 2.3 collective-permute-done.3
  19.3 227.8 %while.62 = (s32[]{:T(128)}, f32[15,4,128]{2,0,1:T(8,128)S(1)}, f32[9,15,4,128]{3,1,2,0:T(8,128)S(1)}, s32[]{:T(128)}, s32[3,26]{1,0:T(4,128)S(1)}, /*index=5*/f...) while((s32[]{:T(128)}, f32[15,4,128]{2,0,1:T(8,128)S(1)}, ...), condition=%wide.region_8.9_spmd, body=%wide.region_2.8_spmd.sunk | while | flops 3182397 | bytes 5304801 | solution.py:178
  247.3 26.1 %collective-permute-start.4 = (f32[3,15,512]{2,1,0:T(8,128)S(1)}, f32[3,15,512]{2,1,0:T(8,128)S(1)}, u32[]{:S(2)}, u32[]{:S(2)}) collective-permute-start(f32[3,15,512]{2,1,0:T(8,128)S(1)} %squeeze.187), channel_id=1, source_target_pairs={{0,16},{16,32},{32,48},{48,64},{64,80},{80,96},{96,112},{112,128},... | collective-permute-start | bytes 276488 | tf_op jit(solution)/shard_map/ppermute | solution.py:21
  273.4 1.9 collective-permute-start.5
  275.5 3.9 collective-permute-done.5
  279.4 1.9 collective-permute-start.6
  281.3 3.4 collective-permute-start.7
  284.7 10.9 %while.63 = (s32[]{:T(128)}, f32[15,4,128]{2,0,1:T(8,128)S(1)}, f32[9,7,4,128]{3,2,1,0:T(4,128)S(1)}, s32[]{:T(128)}, s32[]{:T(128)}, /*index=5*/s32[]{}, s32[]{}, s32[3]{0:T(128)S(1)}, s32[1]{0:T(128)}) while((s32[]{:T(128)}, f32[15,4,128]{2,0,1:T(8,128)S(1)}, f32[9,7,4,128]{3,2,1,0:T(4,128)S(1)}, s32[]{:T(128)}, s32[]{:T(128)}, ...), condition=%wide.region_13.0_spmd, body=%wide.region_9.13_spmd.sunk | while | flops 2688916 | bytes 5255327 | solution.py:160
  296.7 2.4 collective-permute-start.8
  299.1 1.9 collective-permute-start.9
  301.0 3.3 collective-permute-done.9
  304.3 1.9 collective-permute-start.10
  306.2 3.4 collective-permute-start.11
  311.8 209.7 %while.64 = (s32[]{:T(128)}, f32[3,4,128]{2,0,1:T(4,128)S(1)}, f32[9,3,4,128]{3,1,2,0:T(4,128)S(1)}, s32[]{:T(128)}, s32[3,26]{1,0:T(4,128)S(1)}, /*index=5*/f32...) while((s32[]{:T(128)}, f32[3,4,128]{2,0,1:T(4,128)S(1)}, ...), condition=%wide.region_21.0_spmd, body=%wide.region_15.0_spmd.sunk | while | flops 1115462 | bytes 1571489 | solution.py:178
  521.5 24.0 %collective-permute-start.12 = (f32[3,3,512]{2,1,0:T(4,128)S(1)}, f32[3,3,512]{2,1,0:T(4,128)S(1)}, u32[]{:S(2)}, u32[]{:S(2)}) collective-permute-start(f32[3,3,512]{2,1,0:T(4,128)S(1)} %get-tuple-element.613), channel_id=1, source_target_pairs={{0,16},{16,32},{32,48},{48,64},{64,80},{80,96},{96,112},{112,128},... | collective-permute-start | bytes 55304 | tf_op jit(solution)/shard_map/ppermute | solution.py:21
  545.5 1.9 collective-permute-start.13
  548.1 2.6 collective-permute-done.13
  552.6 3.4 collective-permute-start.15
  556.0 8.9 %while.65 = (s32[]{:T(128)}, f32[3,4,128]{2,0,1:T(4,128)S(1)}, f32[9,16,4,128]{3,2,1,0:T(4,128)S(1)}, s32[]{:T(128)}, s32[]{:T(128)}, /*index=5*/s32[]{}, s32[]{...) while((s32[]{:T(128)}, f32[3,4,128]{2,0,1:T(4,128)S(1)}, ...), condition=%wide.region_26.0_spmd, body=%wide.region_22.0_spmd.sunk | while | flops 950813 | bytes 1282915 | solution.py:160
  (1085 shorter events, 206.8 us)
Async XLA Ops:
  1.4 14.7 %copy-start.3 = (s32[512]{0:T(512)S(1)}, s32[512]{0:T(512)}, u32[]{:S(2)}) copy-start(s32[512]{0:T(512)} %param.34) | copy-start | bytes 6148
  1.4 14.7 %copy-start.5 = (f32[3]{0:T(128)S(1)}, f32[3]{0:T(128)}, u32[]{:S(2)}) copy-start(f32[3]{0:T(128)} %constant.570.clone) | copy-start | bytes 40
  1.4 14.7 %copy-start.6 = (f32[3]{0:T(128)S(1)}, f32[3]{0:T(128)}, u32[]{:S(2)}) copy-start(f32[3]{0:T(128)} %constant.571.clone) | copy-start | bytes 40
  1.4 14.7 %copy-start.7 = (f32[3]{0:T(128)S(1)}, f32[3]{0:T(128)}, u32[]{:S(2)}) copy-start(f32[3]{0:T(128)} %constant.572.clone) | copy-start | bytes 40
  1.4 6.2 %collective-permute-start = (f32[1,1,7,512]{3,2,1,0:T(8,128)S(1)}, f32[1,1,7,512]{3,2,1,0:T(8,128)S(1)}, u32[]{:S(2)}, u32[]{:S(2)}) collective-permute-start(f32[1,1,7,512]{3,2,1,0:T(8,128)S(1)} %maximum_bitcast_fusion), channel_id=1, source_target_pairs={{0,16},{16,32},{32,48},{48,64},{64,80},{80,96},{96,112},{112,128},... | collective-permute-start | bytes 43016 | tf_op jit(solution)/shard_map/ppermute | solution.py:31
  5.7 5.1 collective-permute-start.1
  10.7 5.4 copy-start.4
  10.7 5.5 collective-permute-start.2
  13.7 4.8 collective-permute-start.3
  18.6 0.7 copy-start
  18.6 0.7 copy-start.1
  247.3 28.2 %collective-permute-start.4 = (f32[3,15,512]{2,1,0:T(8,128)S(1)}, f32[3,15,512]{2,1,0:T(8,128)S(1)}, u32[]{:S(2)}, u32[]{:S(2)}) collective-permute-start(f32[3,15,512]{2,1,0:T(8,128)S(1)} %squeeze.187), channel_id=1, source_target_pairs={{0,16},{16,32},{32,48},{48,64},{64,80},{80,96},{96,112},{112,128},... | collective-permute-start | bytes 276488 | tf_op jit(solution)/shard_map/ppermute | solution.py:21
  273.4 5.9 %collective-permute-start.5 = (f32[3,15,512]{2,1,0:T(8,128)S(1)}, f32[3,15,512]{2,1,0:T(8,128)S(1)}, u32[]{:S(2)}, u32[]{:S(2)}) collective-permute-start(f32[3,15,512]{2,1,0:T(8,128)S(1)} %squeeze.188), channel_id=1, source_target_pairs={{16,0},{32,16},{48,32},{64,48},{80,64},{96,80},{112,96},{128,112},... | collective-permute-start | bytes 276488 | tf_op jit(solution)/shard_map/ppermute | solution.py:21
  279.4 16.2 %collective-permute-start.6 = (f32[15,512]{1,0:T(8,128)S(1)}, f32[15,512]{1,0:T(8,128)S(1)}, u32[]{:S(2)}, u32[]{:S(2)}) collective-permute-start(f32[15,512]{1,0:T(8,128)S(1)} %get-tuple-element.611), channel_id=1, source_target_pairs={{0,1},{1,2},{2,3},{3,4},{4,5},{5,6},{6,7},{7,8},{8,9},{9,10},{10,1... | collective-permute-start | bytes 92168 | tf_op jit(solution)/shard_map/ppermute | solution.py:21
  281.3 14.3 %collective-permute-start.7 = (f32[15,512]{1,0:T(8,128)S(1)}, f32[15,512]{1,0:T(8,128)S(1)}, u32[]{:S(2)}, u32[]{:S(2)}) collective-permute-start(f32[15,512]{1,0:T(8,128)S(1)} %get-tuple-element.612), channel_id=1, source_target_pairs={{1,0},{2,1},{3,2},{4,3},{5,4},{6,5},{7,6},{8,7},{9,8},{10,9},{11,1... | collective-permute-start | bytes 92168 | tf_op jit(solution)/shard_map/ppermute | solution.py:21
  295.7 0.7 copy-start.2
  296.7 4.3 collective-permute-start.8
  299.1 5.2 collective-permute-start.9
  304.3 5.7 %collective-permute-start.10 = (f32[3,1,9,512]{3,2,1,0:T(8,128)S(1)}, f32[3,1,9,512]{3,2,1,0:T(8,128)S(1)}, u32[]{:S(2)}, u32[]{:S(2)}) collective-permute-start(f32[3,1,9,512]{3,2,1,0:T(8,128)S(1)} %pad_maximum_fusion.3), channel_id=1, source_target_pairs={{0,1},{1,2},{2,3},{3,4},{4,5},{5,6},{6,7},{7,8},{8,9},{9,10},{10,1... | collective-permute-start | bytes 165896 | tf_op jit(solution)/shard_map/ppermute | solution.py:31
  306.2 5.4 collective-permute-start.11
  521.5 26.5 %collective-permute-start.12 = (f32[3,3,512]{2,1,0:T(4,128)S(1)}, f32[3,3,512]{2,1,0:T(4,128)S(1)}, u32[]{:S(2)}, u32[]{:S(2)}) collective-permute-start(f32[3,3,512]{2,1,0:T(4,128)S(1)} %get-tuple-element.613), channel_id=1, source_target_pairs={{0,16},{16,32},{32,48},{48,64},{64,80},{80,96},{96,112},{112,128},... | collective-permute-start | bytes 55304 | tf_op jit(solution)/shard_map/ppermute | solution.py:21
  545.5 5.1 collective-permute-start.13
  550.7 14.2 %collective-permute-start.14 = (f32[3,512]{1,0:T(4,128)S(1)}, f32[3,512]{1,0:T(4,128)S(1)}, u32[]{:S(2)}, u32[]{:S(2)}) collective-permute-start(f32[3,512]{1,0:T(4,128)S(1)} %get-tuple-element.615), channel_id=1, source_target_pairs={{0,1},{1,2},{2,3},{3,4},{4,5},{5,6},{6,7},{7,8},{8,9},{9,10},{10,1... | collective-permute-start | bytes 18440 | tf_op jit(solution)/shard_map/ppermute | solution.py:21
  552.6 12.3 %collective-permute-start.15 = (f32[3,512]{1,0:T(4,128)S(1)}, f32[3,512]{1,0:T(4,128)S(1)}, u32[]{:S(2)}, u32[]{:S(2)}) collective-permute-start(f32[3,512]{1,0:T(4,128)S(1)} %get-tuple-element.616), channel_id=1, source_target_pairs={{1,0},{2,1},{3,2},{4,3},{5,4},{6,5},{7,6},{8,7},{9,8},{10,9},{11,1... | collective-permute-start | bytes 18440 | tf_op jit(solution)/shard_map/ppermute | solution.py:21
where the time goes:
time: 573 us; the launch traced here: 565 us
  loops' own time  259 us (45%)
  other arithmetic  173 us (30%)
  starting transfers between devices  85.5 us (15%)
  local copies, waits for them, and re-layouts  29.8 us (5%)
  waiting for transfers between devices  17.2 us (3%)
    another operation x2, loops' own time, listed_sums(): lax.fori_loop(0, total, listed_visit, (home_acc, far_acc))  258 us
    another operation x88, other arithmetic  66.6 us
    ppermute x8, starting transfers between devices, passed_along(): return lax.ppermute(block, axis, route)  64.5 us
    scatter-add x40, other arithmetic, listed_visit(): home_part = home_part.at[:, first].add(home)  28 us
    dynamic_slice x40, local copies, waits for them, and re-layouts, listed_visit(): second = lists[1, slot]  25.3 us
    scatter-add x40, other arithmetic, listed_visit(): far_part = far_part.at[where_dir, :, second].add(far)  24.3 us
    while x336, other arithmetic  15.3 us
  transfers between devices with their start and end apart: 16, of which 7 were waited for; matrix products, arithmetic and copies ran while one was open for 4% of the time, Pallas kernels for 0%

commit v1 on v0

v1 whole, which is shorter than its diff:
```python
import functools

import jax
import jax.numpy as jnp
from jax import lax
from jax.experimental import pallas as pl
from jax.experimental.pallas import tpu as pltpu
from jax.sharding import PartitionSpec as P

BLOCK = 128
COMPS = 16
SHIFT = 0.1
SYM = ((0, 0), (1, 1), (2, 2), (0, 1), (0, 2), (1, 2))
DIRS = tuple((dx, dy) for dx in (-1, 0, 1) for dy in (-1, 0, 1) if (dx, dy) != (0, 0))
MESH = pl.DeviceIdType.MESH
F32 = jnp.float32


def exact_product(values, onehot, contract):
    high = values.astype(jnp.bfloat16)
    rest = values - high.astype(F32)
    mid = rest.astype(jnp.bfloat16)
    low = (rest - mid.astype(F32)).astype(jnp.bfloat16)
    parts = jnp.concatenate([high, mid, low], axis=0)
    out = lax.dot_general(parts, onehot, (((1,), (contract,)), ((), ())), preferred_element_type=F32)
    return out[0:16] + out[16:32] + out[32:48]


def send_range(step):
    if step == 0:
        return (1, 2), 1
    return ((2, 1), 0) if step == 1 else ((1, 1), 3)


def constitutive(moment, strain_sum, plastic, material):
    m00, m11, m22 = moment[0] + SHIFT, moment[1] + SHIFT, moment[2] + SHIFT
    m01, m02, m12 = moment[3:6]
    c00 = m11 * m22 - m12 * m12
    c01 = m02 * m12 - m01 * m22
    c02 = m01 * m12 - m02 * m11
    c11 = m00 * m22 - m02 * m02
    c12 = m01 * m02 - m00 * m12
    c22 = m00 * m11 - m01 * m01
    inverse = 1.0 / (m00 * c00 + m01 * c01 + m02 * c02)
    c00, c01, c02, c11, c12, c22 = [inverse * c for c in (c00, c01, c02, c11, c12, c22)]
    correct = [[c00, c01, c02], [c01, c11, c12], [c02, c12, c22]]
    grad = [
        [sum(strain_sum[3 * a + k] * correct[k][b] for k in range(3)) for b in range(3)]
        for a in range(3)
    ]
    strain = [0.5 * (grad[a][b] + grad[b][a]) - plastic[s] for s, (a, b) in enumerate(SYM)]
    first, second = material == 0.0, material == 1.0
    shear = jnp.where(first, 30.0, jnp.where(second, 40.0, 60.0))
    bulk = jnp.where(first, 60.0, jnp.where(second, 80.0, 120.0))
    yield_stress = jnp.where(first, 1.0, jnp.where(second, 1.4, 2.2))
    trace = strain[0] + strain[1] + strain[2]
    third = trace * (1.0 / 3.0)
    dev = [strain[s] - third if s < 3 else strain[s] for s in range(6)]
    trial = [2.0 * shear * value for value in dev]
    squares = (trial[0] ** 2 + trial[1] ** 2 + trial[2] ** 2) + 2.0 * (
        trial[3] ** 2 + trial[4] ** 2 + trial[5] ** 2
    )
    factor = yield_stress / jnp.maximum(jnp.sqrt(1.5 * squares), yield_stress)
    plastic_new = [plastic[s] + (1.0 - factor) * dev[s] for s in range(6)]
    pressure = bulk * trace
    s0, s1, s2, s3, s4, s5 = [
        factor * trial[s] + pressure if s < 3 else factor * trial[s] for s in range(6)
    ]
    full = [[s0, s3, s4], [s3, s1, s5], [s4, s5, s2]]
    piola = [
        full[a][0] * correct[0][b] + full[a][1] * correct[1][b] + full[a][2] * correct[2][b]
        for a in range(3)
        for b in range(3)
    ]
    return piola, plastic_new


def kernel(
    n_gx,
    n_gy,
    ref_ref,
    disp_ref,
    vol_ref,
    plastic_ref,
    material_ref,
    force_ref,
    plastic_out_ref,
    packed,
    onehots,
    region,
    state,
    rolled,
    weights,
    piolas,
    rolled_piolas,
    results,
    send_sem,
    recv_sem,
):
    gx = lax.axis_index("gx")
    gy = lax.axis_index("gy")

    def present(dx, dy):
        conditions = []
        if dx:
            conditions.append(gx < n_gx - 1 if dx > 0 else gx > 0)
        if dy:
            conditions.append(gy < n_gy - 1 if dy > 0 else gy > 0)
        return functools.reduce(jnp.logical_and, conditions)

    for rx in range(4):
        for ry in range(4):
            if rx in (0, 3) or ry in (0, 3):
                region[rx, ry] = jnp.zeros((COMPS, BLOCK), F32)

    barrier = pltpu.get_barrier_semaphore()
    for dx, dy in DIRS:

        @pl.when(present(dx, dy))
        def _():
            pl.semaphore_signal(
                barrier, inc=1, device_id={"gx": gx + dx, "gy": gy + dy}, device_id_type=MESH
            )

    row_index = lax.broadcasted_iota(jnp.int32, (BLOCK, BLOCK), 0).astype(F32)
    for block in range(4):
        lanes = pl.ds(block * BLOCK, BLOCK)
        packed[block, 0:3, :] = ref_ref[:, lanes]
        packed[block, 3:6, :] = disp_ref[:, lanes]
        packed[block, 6:7, :] = vol_ref[:, lanes]
        packed[block, 7:13, :] = plastic_ref[:, lanes]
        packed[block, 13:14, :] = material_ref[:, lanes].astype(F32)
        packed[block, 14:16, :] = jnp.zeros((2, BLOCK), F32)
        near = jnp.floor(ref_ref[:, lanes] + 0.5)
        near = near - jnp.min(near, axis=1, keepdims=True)
        site = near[0:1] * 32.0 + near[1:2] * 8.0 + near[2:3]
        onehot = jnp.where(row_index == site, 1.0, 0.0).astype(jnp.bfloat16)
        onehots[block] = onehot
        region[1 + block // 2, 1 + block % 2] = exact_product(packed[block], onehot, 1)

    beside = [
        1 + (place > 0).astype(jnp.int32) + (place < size - 1).astype(jnp.int32)
        for place, size in ((gx, n_gx), (gy, n_gy))
    ]
    pl.semaphore_wait(barrier, beside[0] * beside[1] - 1)

    def copy_to(number):
        dx, dy = DIRS[number]
        (sx, nx), tx = send_range(dx)
        (sy, ny), ty = send_range(dy)
        return pltpu.make_async_remote_copy(
            src_ref=region.at[pl.ds(sx, nx), pl.ds(sy, ny)],
            dst_ref=region.at[pl.ds(tx, nx), pl.ds(ty, ny)],
            send_sem=send_sem.at[number],
            recv_sem=recv_sem.at[number],
            device_id={"gx": gx + dx, "gy": gy + dy},
            device_id_type=MESH,
        )

    for number, (dx, dy) in enumerate(DIRS):

        @pl.when(present(dx, dy))
        def _():
            copy_to(number).start()

    for number, (dx, dy) in enumerate(DIRS):

        @pl.when(present(-dx, -dy))
        def _():
            copy_to(number).wait_recv()

    chunk = lax.broadcasted_iota(jnp.int32, (COMPS, BLOCK), 1) // 32
    for rx in range(4):
        blocks = [region[rx, ry] for ry in range(4)]
        for x in range(4):
            turned = [
                pltpu.roll(blocks[ry], 32 * (ry - x) % 128, 1) if ry != x else blocks[ry]
                for ry in range(4)
            ]
            low = jnp.where(chunk == 0, turned[0], turned[1])
            high = jnp.where(chunk == 2, turned[2], turned[3])
            value = jnp.where(chunk < 2, low, high)
            row = (rx * 4 + x + 4) % 16
            state[pl.ds(row, COMPS, stride=16), :] = value

    def piece(comp, part):
        return state[pl.ds(comp * 16 + part * 8, 8), :]

    z_lane = lax.broadcasted_iota(jnp.int32, (8, BLOCK), 1) % 8
    home = [[piece(c, part) for c in range(3)] for part in range(2)]

    def lane_shift(index):
        sy, sz = index // 5 - 2, index % 5 - 2
        return lax.rem(256 - (8 * sy + sz), 128), sz

    def moment_visit(index, sums):
        shift, sz = lane_shift(index)
        inside = (z_lane + sz >= 0) & (z_lane + sz < 8)
        reach = jnp.where(inside, 2.0, -100.0)
        for c in range(7):
            scale = 1.5 / 8.0 if c == 6 else None
            for part in range(2):
                value = piece(c, part)
                if scale is not None:
                    value = value * scale
                value = pltpu.roll(value, shift, 1)
                rolled[pl.ds(c * 32 + part * 8, 8), :] = value
                rolled[pl.ds(c * 32 + part * 8 + 16, 8), :] = value
        sums = [list(s) for s in sums]
        for sx in range(-2, 3):
            for part in range(2):
                base = 8 if part == 1 else 16
                other = [rolled[pl.ds(c * 32 + base + sx, 8), :] for c in range(7)]
                dX = [other[a] - home[part][a] for a in range(3)]
                square = dX[0] * dX[0] + dX[1] * dX[1] + dX[2] * dX[2]
                dist = square * lax.rsqrt(jnp.maximum(square, 1e-20))
                t = jnp.maximum(reach - dist, 0.0)
                w = (other[6] * t) * (t * t)
                g = [w * dX[a] for a in range(3)]
                acc = sums[part]
                for s, (a, b) in enumerate(SYM):
                    acc[s] = acc[s] + g[a] * dX[b]
                for a in range(3):
                    for b in range(3):
                        acc[6 + 3 * a + b] = acc[6 + 3 * a + b] + other[3 + a] * g[b]
                for a in range(3):
                    acc[15 + a] = acc[15 + a] + g[a]
                if part == 1:
                    for a in range(3):
                        weights[index, (sx + 2) * 3 + a] = g[a]
        return tuple(tuple(s) for s in sums)

    zero = jnp.zeros((8, BLOCK), F32)
    sums = lax.fori_loop(0, 25, moment_visit, tuple((zero,) * 18 for _ in range(2)))

    own_piola, own_plastic = None, None
    for part in range(2):
        acc = sums[part]
        disp = [piece(3 + a, part) for a in range(3)]
        strain_sum = [acc[6 + 3 * a + b] - disp[a] * acc[15 + b] for a in range(3) for b in range(3)]
        plastic = [piece(7 + s, part) for s in range(6)]
        piola, plastic_new = constitutive(acc[0:6], strain_sum, plastic, piece(13, part))
        for c in range(9):
            piolas[c, pl.ds(part * 8, 8), :] = piola[c]
        if part == 1:
            own_piola, own_plastic = piola, plastic_new
    for s in range(6):
        results[pl.ds((3 + s) * 8, 8), :] = own_plastic[s]
    lean = sums[1][15:18]
    start = tuple(sum(own_piola[3 * a + b] * lean[b] for b in range(3)) for a in range(3))

    def force_visit(index, force):
        shift, _ = lane_shift(index)
        for c in range(9):
            ring = pltpu.roll(piolas[c, 0:8, :], shift, 1)
            rolled_piolas[pl.ds(c * 24, 8), :] = ring
            rolled_piolas[pl.ds(c * 24 + 8, 8), :] = pltpu.roll(piolas[c, 8:16, :], shift, 1)
            rolled_piolas[pl.ds(c * 24 + 16, 8), :] = ring
        force = list(force)
        for sx in range(-2, 3):
            g = [weights[index, (sx + 2) * 3 + a] for a in range(3)]
            for a in range(3):
                for b in range(3):
                    other = rolled_piolas[pl.ds((3 * a + b) * 24 + 8 + sx, 8), :]
                    force[a] = force[a] + other * g[b]
        return tuple(force)

    force = lax.fori_loop(0, 25, force_visit, start)
    volume = piece(6, 1)
    for a in range(3):
        results[pl.ds(a * 8, 8), :] = volume * force[a]
    for c in range(9, 16):
        results[pl.ds(c * 8, 8), :] = zero

    for bx in range(2):
        rows = [results[pl.ds(bx * 4 + x, COMPS, stride=8), :] for x in range(4)]
        for by in range(2):
            block = bx * 2 + by
            turned = [pltpu.roll(rows[x], 32 * (x - by - 1) % 128, 1) for x in range(4)]
            low = jnp.where(chunk == 0, turned[0], turned[1])
            high = jnp.where(chunk == 2, turned[2], turned[3])
            value = exact_product(jnp.where(chunk < 2, low, high), onehots[block], 0)
            lanes = pl.ds(block * BLOCK, BLOCK)
            force_ref[:, lanes] = value[0:3]
            plastic_out_ref[:, lanes] = value[3:9]

    for number, (dx, dy) in enumerate(DIRS):

        @pl.when(present(dx, dy))
        def _():
            copy_to(number).wait_send()


def solution(mesh):
    n_gx, n_gy = mesh.shape["gx"], mesh.shape["gy"]

    def on_device(ref_pos, disp, volume, plastic, material, pair_list, pair_count):
        count = ref_pos.shape[1]
        vmem = pl.BlockSpec(memory_space=pltpu.VMEM)
        return pl.pallas_call(
            functools.partial(kernel, n_gx, n_gy),
            out_shape=(
                jax.ShapeDtypeStruct((3, count), F32),
                jax.ShapeDtypeStruct((6, count), F32),
            ),
            in_specs=[vmem] * 5,
            out_specs=(vmem, vmem),
            scratch_shapes=[
                pltpu.VMEM((4, COMPS, BLOCK), F32),
                pltpu.VMEM((4, BLOCK, BLOCK), jnp.bfloat16),
                pltpu.VMEM((4, 4, COMPS, BLOCK), F32),
                pltpu.VMEM((COMPS * 16, BLOCK), F32),
                pltpu.VMEM((7 * 32, BLOCK), F32),
                pltpu.VMEM((25, 15, 8, BLOCK), F32),
                pltpu.VMEM((9, 16, BLOCK), F32),
                pltpu.VMEM((9 * 24, BLOCK), F32),
                pltpu.VMEM((COMPS * 8, BLOCK), F32),
                pltpu.SemaphoreType.DMA((8,)),
                pltpu.SemaphoreType.DMA((8,)),
            ],
            compiler_params=pltpu.CompilerParams(collective_id=0, has_side_effects=True),
        )(ref_pos, disp, volume.reshape(1, count), plastic, material.reshape(1, count))

    in_specs = (
        P(None, ("gx", "gy")),
        P(None, ("gx", "gy")),
        P(("gx", "gy")),
        P(None, ("gx", "gy")),
        P(("gx", "gy")),
        P(("gx", "gy"), None, None),
        P(("gx", "gy")),
    )
    out_specs = (P(None, ("gx", "gy")), P(None, ("gx", "gy")))
    return jax.shard_map(
        on_device, mesh=mesh, in_specs=in_specs, out_specs=out_specs, check_vma=False
    )
```

time: 573 us -> 20.7 us (0.04)
  the two profiles are of different devices: /device:TPU:17 before, /device:TPU:103 now
where the time goes in v1:
time: 20.7 us; the launch traced here: 20.5 us
  Pallas kernels  17.9 us (86%)
  local copies, waits for them, and re-layouts  1.91 us (9%)
  between operations  0.65 us (3%)
    pallas_call x1, Pallas kernels, on_device(): pl.pallas_call(functools.partial(kernel, n_gx, n_gy), out_shape=(jax.Shap...  17.9 us
    unnamed x4, local copies, waits for them, and re-layouts  1.91 us

profile of v1, /device:TPU:103, one launch (start us, length us, event | category | flops | bytes accessed | tf_op | source)
XLA Modules:
  0.0 20.5 jit_solution(14045124831957244463)
XLA Ops:
  0.6 17.9 %shard_map.68 = (f32[3,512]{1,0:T(4,128)}, f32[6,512]{1,0:T(8,128)}) custom-call(f32[3,512]{1,0:T(4,128)} %ref_ref.1, f32[3,512]{1,0:T(4,128)} %disp_ref.1, f32[1,512]{1,0:T(1,128)} %bitcast.2, f32[6,512]{1,0:T(8,128)} %plastic_ref.1, s32[1,512]{1,0:T(1,128)} %bitcast.3), custom_call_target="tpu_custom_call" | custom-call | tf_op jit(solution)/shard_map/pallas_call | solution.py:300
  18.6 0.0 copy-start
  18.6 1.3 %copy.9 = f32[3,512]{1,0:T(4,128)} copy(f32[3,512]{1,0:T(4,128)} %get-tuple-element.4) | data formatting | bytes 12288
  19.9 0.0 copy-done
  19.9 0.6 %copy.10 = f32[6,512]{1,0:T(8,128)} copy(f32[6,512]{1,0:T(8,128)S(1)} %copy-done) | data formatting | bytes 24576
Async XLA Ops:
  18.6 1.3 %copy-start = (f32[6,512]{1,0:T(8,128)S(1)}, f32[6,512]{1,0:T(8,128)}, u32[]{:S(2)}) copy-start(f32[6,512]{1,0:T(8,128)} %get-tuple-element.5) | copy-start | bytes 36868

commit v2 on v1

--- a/solution.py
+++ b/solution.py
@@ -13,6 +13,16 @@
 SYM = ((0, 0), (1, 1), (2, 2), (0, 1), (0, 2), (1, 2))
 DIRS = tuple((dx, dy) for dx in (-1, 0, 1) for dy in (-1, 0, 1) if (dx, dy) != (0, 0))
 MESH = pl.DeviceIdType.MESH
+
+
+def within_reach(sx, sy, sz):
+    return sum(max(abs(step) - 0.6, 0.0) ** 2 for step in (sx, sy, sz)) < 4.0
+
+
+STEPS = range(-2, 3)
+OFFSETS = tuple(
+    (sy, sz, tuple(sx for sx in STEPS if within_reach(sx, sy, sz))) for sy in STEPS for sz in STEPS
+)
 F32 = jnp.float32
 
 
@@ -189,28 +199,23 @@
     z_lane = lax.broadcasted_iota(jnp.int32, (8, BLOCK), 1) % 8
     home = [[piece(c, part) for c in range(3)] for part in range(2)]
 
-    def lane_shift(index):
-        sy, sz = index // 5 - 2, index % 5 - 2
-        return lax.rem(256 - (8 * sy + sz), 128), sz
-
-    def moment_visit(index, sums):
-        shift, sz = lane_shift(index)
+    def moment_visit(slot, sy, sz, x_steps, sums):
+        shift = -(8 * sy + sz) % 128
         inside = (z_lane + sz >= 0) & (z_lane + sz < 8)
         reach = jnp.where(inside, 2.0, -100.0)
         for c in range(7):
-            scale = 1.5 / 8.0 if c == 6 else None
             for part in range(2):
-                value = piece(c, part)
-                if scale is not None:
-                    value = value * scale
-                value = pltpu.roll(value, shift, 1)
-                rolled[pl.ds(c * 32 + part * 8, 8), :] = value
-                rolled[pl.ds(c * 32 + part * 8 + 16, 8), :] = value
-        sums = [list(s) for s in sums]
-        for sx in range(-2, 3):
+                value = scaled[part] if c == 6 else piece(c, part)
+                if shift:
+                    value = pltpu.roll(value, shift, 1)
+                rolled[slot, pl.ds(c * 32 + part * 8, 8), :] = value
+                rolled[slot, pl.ds(c * 32 + part * 8 + 16, 8), :] = value
+        for sx in x_steps:
+            if (sx, sy, sz) == (0, 0, 0):
+                continue
             for part in range(2):
                 base = 8 if part == 1 else 16
-                other = [rolled[pl.ds(c * 32 + base + sx, 8), :] for c in range(7)]
+                other = [rolled[slot, pl.ds(c * 32 + base + sx, 8), :] for c in range(7)]
                 dX = [other[a] - home[part][a] for a in range(3)]
                 square = dX[0] * dX[0] + dX[1] * dX[1] + dX[2] * dX[2]
                 dist = square * lax.rsqrt(jnp.maximum(square, 1e-20))
@@ -227,11 +232,13 @@
                     acc[15 + a] = acc[15 + a] + g[a]
                 if part == 1:
                     for a in range(3):
-                        weights[index, (sx + 2) * 3 + a] = g[a]
-        return tuple(tuple(s) for s in sums)
+                        weights[slot, (sx + 2) * 3 + a] = g[a]
 
     zero = jnp.zeros((8, BLOCK), F32)
-    sums = lax.fori_loop(0, 25, moment_visit, tuple((zero,) * 18 for _ in range(2)))
+    scaled = [piece(6, part) * (1.5 / 8.0) for part in range(2)]
+    sums = [[zero] * 18 for _ in range(2)]
+    for slot, (sy, sz, x_steps) in enumerate(OFFSETS):
+        moment_visit(slot, sy, sz, x_steps, sums)
 
     own_piola, own_plastic = None, None
     for part in range(2):
@@ -247,25 +254,26 @@
     for s in range(6):
         results[pl.ds((3 + s) * 8, 8), :] = own_plastic[s]
     lean = sums[1][15:18]
-    start = tuple(sum(own_piola[3 * a + b] * lean[b] for b in range(3)) for a in range(3))
-
-    def force_visit(index, force):
-        shift, _ = lane_shift(index)
+    force = [sum(own_piola[3 * a + b] * lean[b] for b in range(3)) for a in range(3)]
+
+    for slot, (sy, sz, x_steps) in enumerate(OFFSETS):
+        shift = -(8 * sy + sz) % 128
         for c in range(9):
-            ring = pltpu.roll(piolas[c, 0:8, :], shift, 1)
-            rolled_piolas[pl.ds(c * 24, 8), :] = ring
-            rolled_piolas[pl.ds(c * 24 + 8, 8), :] = pltpu.roll(piolas[c, 8:16, :], shift, 1)
-            rolled_piolas[pl.ds(c * 24 + 16, 8), :] = ring
-        force = list(force)
-        for sx in range(-2, 3):
-            g = [weights[index, (sx + 2) * 3 + a] for a in range(3)]
+            ring, inner = piolas[c, 0:8, :], piolas[c, 8:16, :]
+            if shift:
+                ring, inner = pltpu.roll(ring, shift, 1), pltpu.roll(inner, shift, 1)
+            rolled_piolas[slot, pl.ds(c * 24, 8), :] = ring
+            rolled_piolas[slot, pl.ds(c * 24 + 8, 8), :] = inner
+            rolled_piolas[slot, pl.ds(c * 24 + 16, 8), :] = ring
+        for sx in x_steps:
+            if (sx, sy, sz) == (0, 0, 0):
+                continue
+            g = [weights[slot, (sx + 2) * 3 + a] for a in range(3)]
             for a in range(3):
                 for b in range(3):
-                    other = rolled_piolas[pl.ds((3 * a + b) * 24 + 8 + sx, 8), :]
+                    other = rolled_piolas[slot, pl.ds((3 * a + b) * 24 + 8 + sx, 8), :]
                     force[a] = force[a] + other * g[b]
-        return tuple(force)
-
-    force = lax.fori_loop(0, 25, force_visit, start)
+
     volume = piece(6, 1)
     for a in range(3):
         results[pl.ds(a * 8, 8), :] = volume * force[a]
@@ -310,10 +318,10 @@
                 pltpu.VMEM((4, BLOCK, BLOCK), jnp.bfloat16),
                 pltpu.VMEM((4, 4, COMPS, BLOCK), F32),
                 pltpu.VMEM((COMPS * 16, BLOCK), F32),
-                pltpu.VMEM((7 * 32, BLOCK), F32),
+                pltpu.VMEM((25, 7 * 32, BLOCK), F32),
                 pltpu.VMEM((25, 15, 8, BLOCK), F32),
                 pltpu.VMEM((9, 16, BLOCK), F32),
-                pltpu.VMEM((9 * 24, BLOCK), F32),
+                pltpu.VMEM((25, 9 * 24, BLOCK), F32),
                 pltpu.VMEM((COMPS * 8, BLOCK), F32),
                 pltpu.SemaphoreType.DMA((8,)),
                 pltpu.SemaphoreType.DMA((8,)),

time: 20.7 us -> 15.6 us (0.75)
  Pallas kernels: 17.9 us -> 12.8 us
    pallas_call x1, Pallas kernels: 17.9 us -> 12.8 us  [on_device(): pl.pallas_call(functools.partial(kernel, n_gx, n_gy), out_shape=(jax.Shap...]
where the time goes in v2:
time: 15.6 us; the launch traced here: 15.4 us
  Pallas kernels  12.8 us (82%)
  local copies, waits for them, and re-layouts  1.91 us (12%)
  between operations  0.65 us (4%)
    pallas_call x1, Pallas kernels, on_device(): pl.pallas_call(functools.partial(kernel, n_gx, n_gy), out_shape=(jax.Shap...  12.8 us
    unnamed x4, local copies, waits for them, and re-layouts  1.91 us

profile of v2, /device:TPU:103, one launch (start us, length us, event | category | flops | bytes accessed | tf_op | source)
XLA Modules:
  0.0 15.4 jit_solution(8151408050378320649)
XLA Ops:
  0.6 12.8 %shard_map.68 = (f32[3,512]{1,0:T(4,128)}, f32[6,512]{1,0:T(8,128)}) custom-call(f32[3,512]{1,0:T(4,128)} %ref_ref.1, f32[3,512]{1,0:T(4,128)} %disp_ref.1, f32[1,512]{1,0:T(1,128)} %bitcast.2, f32[6,512]{1,0:T(8,128)} %plastic_ref.1, s32[1,512]{1,0:T(1,128)} %bitcast.3), custom_call_target="tpu_custom_call" | custom-call | tf_op jit(solution)/shard_map/pallas_call | solution.py:308
  13.5 0.0 copy-start
  13.5 1.3 %copy.9 = f32[3,512]{1,0:T(4,128)} copy(f32[3,512]{1,0:T(4,128)} %get-tuple-element.4) | data formatting | bytes 12288
  14.8 0.0 copy-done
  14.8 0.6 %copy.10 = f32[6,512]{1,0:T(8,128)} copy(f32[6,512]{1,0:T(8,128)S(1)} %copy-done) | data formatting | bytes 24576
Async XLA Ops:
  13.5 1.3 %copy-start = (f32[6,512]{1,0:T(8,128)S(1)}, f32[6,512]{1,0:T(8,128)}, u32[]{:S(2)}) copy-start(f32[6,512]{1,0:T(8,128)} %get-tuple-element.5) | copy-start | bytes 36868

commit v3 on v2

--- a/solution.py
+++ b/solution.py
@@ -85,28 +85,40 @@
     return piola, plastic_new
 
 
-def kernel(
+def exchange_kernel(
     n_gx,
     n_gy,
+    ref_hbm,
+    disp_hbm,
+    vol_hbm,
+    plastic_hbm,
+    material_hbm,
+    region,
+    onehots,
     ref_ref,
     disp_ref,
     vol_ref,
     plastic_ref,
     material_ref,
-    force_ref,
-    plastic_out_ref,
     packed,
-    onehots,
-    region,
-    state,
-    rolled,
-    weights,
-    piolas,
-    rolled_piolas,
-    results,
+    load_sem,
     send_sem,
     recv_sem,
 ):
+    loads = [
+        pltpu.make_async_copy(source, target, load_sem.at[number])
+        for number, (source, target) in enumerate(
+            (
+                (ref_hbm, ref_ref),
+                (disp_hbm, disp_ref),
+                (vol_hbm, vol_ref),
+                (plastic_hbm, plastic_ref),
+                (material_hbm, material_ref),
+            )
+        )
+    ]
+    for load in loads:
+        load.start()
     gx = lax.axis_index("gx")
     gy = lax.axis_index("gy")
 
@@ -131,6 +143,9 @@
             pl.semaphore_signal(
                 barrier, inc=1, device_id={"gx": gx + dx, "gy": gy + dy}, device_id_type=MESH
             )
+
+    for load in loads:
+        load.wait()
 
     row_index = lax.broadcasted_iota(jnp.int32, (BLOCK, BLOCK), 0).astype(F32)
     for block in range(4):
@@ -179,6 +194,25 @@
         def _():
             copy_to(number).wait_recv()
 
+    for number, (dx, dy) in enumerate(DIRS):
+
+        @pl.when(present(dx, dy))
+        def _():
+            copy_to(number).wait_send()
+
+
+def stencil_kernel(
+    region,
+    onehots,
+    force_ref,
+    plastic_out_ref,
+    state,
+    rolled,
+    weights,
+    piolas,
+    rolled_piolas,
+    results,
+):
     chunk = lax.broadcasted_iota(jnp.int32, (COMPS, BLOCK), 1) // 32
     for rx in range(4):
         blocks = [region[rx, ry] for ry in range(4)]
@@ -292,12 +326,6 @@
             force_ref[:, lanes] = value[0:3]
             plastic_out_ref[:, lanes] = value[3:9]
 
-    for number, (dx, dy) in enumerate(DIRS):
-
-        @pl.when(present(dx, dy))
-        def _():
-            copy_to(number).wait_send()
-
 
 def solution(mesh):
     n_gx, n_gy = mesh.shape["gx"], mesh.shape["gy"]
@@ -305,29 +333,53 @@
     def on_device(ref_pos, disp, volume, plastic, material, pair_list, pair_count):
         count = ref_pos.shape[1]
         vmem = pl.BlockSpec(memory_space=pltpu.VMEM)
+        inputs = [
+            pltpu.with_memory_space_constraint(array, pltpu.HBM)
+            for array in (
+                ref_pos, disp, volume.reshape(1, count), plastic, material.reshape(1, count)
+            )
+        ]
+        region, onehots = pl.pallas_call(
+            functools.partial(exchange_kernel, n_gx, n_gy),
+            out_shape=(
+                jax.ShapeDtypeStruct((4, 4, COMPS, BLOCK), F32),
+                jax.ShapeDtypeStruct((4, BLOCK, BLOCK), jnp.bfloat16),
+            ),
+            in_specs=[pl.BlockSpec(memory_space=pltpu.HBM)] * 5,
+            out_specs=(vmem, vmem),
+            scratch_shapes=[
+                pltpu.VMEM((3, count), F32),
+                pltpu.VMEM((3, count), F32),
+                pltpu.VMEM((1, count), F32),
+                pltpu.VMEM((6, count), F32),
+                pltpu.VMEM((1, count), jnp.int32),
+                pltpu.VMEM((4, COMPS, BLOCK), F32),
+                pltpu.SemaphoreType.DMA((5,)),
+                pltpu.SemaphoreType.DMA((8,)),
+                pltpu.SemaphoreType.DMA((8,)),
+            ],
+            compiler_params=pltpu.CompilerParams(
+                collective_id=0, has_side_effects=True, vmem_limit_bytes=4 << 20
+            ),
+        )(*inputs)
         return pl.pallas_call(
-            functools.partial(kernel, n_gx, n_gy),
+            stencil_kernel,
             out_shape=(
                 jax.ShapeDtypeStruct((3, count), F32),
                 jax.ShapeDtypeStruct((6, count), F32),
             ),
-            in_specs=[vmem] * 5,
+            in_specs=[vmem] * 2,
             out_specs=(vmem, vmem),
             scratch_shapes=[
-                pltpu.VMEM((4, COMPS, BLOCK), F32),
-                pltpu.VMEM((4, BLOCK, BLOCK), jnp.bfloat16),
-                pltpu.VMEM((4, 4, COMPS, BLOCK), F32),
                 pltpu.VMEM((COMPS * 16, BLOCK), F32),
                 pltpu.VMEM((25, 7 * 32, BLOCK), F32),
                 pltpu.VMEM((25, 15, 8, BLOCK), F32),
                 pltpu.VMEM((9, 16, BLOCK), F32),
                 pltpu.VMEM((25, 9 * 24, BLOCK), F32),
                 pltpu.VMEM((COMPS * 8, BLOCK), F32),
-                pltpu.SemaphoreType.DMA((8,)),
-                pltpu.SemaphoreType.DMA((8,)),
             ],
-            compiler_params=pltpu.CompilerParams(collective_id=0, has_side_effects=True),
-        )(ref_pos, disp, volume.reshape(1, count), plastic, material.reshape(1, count))
+            compiler_params=pltpu.CompilerParams(vmem_limit_bytes=16 << 20),
+        )(region, onehots)
 
     in_specs = (
         P(None, ("gx", "gy")),

time: 15.6 us -> 13.1 us (0.84)
  local copies, waits for them, and re-layouts: 1.91 us -> 0 us
  Pallas kernels: 12.8 us -> 12.3 us
    unnamed x4 -> x0, local copies, waits for them, and re-layouts: 1.91 us -> none
    pallas_call x1 -> x2, Pallas kernels: 12.8 us -> 12.3 us  [the longest x1 9.12 us: on_device(): pl.pallas_call(functools.partial(exchange_kernel, n_gx, n_gy), out_shape=...]
where the time goes in v3:
time: 13.1 us; the launch traced here: 13 us
  Pallas kernels  12.3 us (94%)
  between operations  0.64 us (5%)
    pallas_call x1, Pallas kernels, on_device(): pl.pallas_call(functools.partial(exchange_kernel, n_gx, n_gy), out_shape=...  9.12 us
    pallas_call x1, Pallas kernels, on_device(): pl.pallas_call(stencil_kernel, out_shape=(jax.ShapeDtypeStruct((3, count)...  3.19 us

profile of v3, /device:TPU:103, one launch (start us, length us, event | category | flops | bytes accessed | tf_op | source)
XLA Modules:
  0.0 13.0 jit_solution(2505519759226332106)
XLA Ops:
  0.6 9.1 %shard_map.68 = (f32[4,4,16,128]{3,2,1,0:T(8,128)S(1)}, bf16[4,128,128]{2,1,0:T(8,128)(2,1)S(1)}) custom-call(f32[3,512]{1,0:T(4,128)} %ref_hbm.1, f32[3,512]{1,0:T(4,128)} %disp_hbm.1, f32[1,512]{1,0:T(1,128)} %bitcast.2, f32[6,512]{1,0:T(8,128)} %plastic_hbm.1, s32[1,512]{1,0:T(1,128)} %bitcast.3), custom_call_target="tpu_custom_call" | custom-call | tf_op jit(solution)/shard_map/pallas_call | solution.py:342
  9.8 3.2 %shard_map.69 = (f32[3,512]{1,0:T(4,128)}, f32[6,512]{1,0:T(8,128)}) custom-call(f32[4,4,16,128]{3,2,1,0:T(8,128)S(1)} %get-tuple-element.4.region, bf16[4,128,128]{2,1,0:T(8,128)(2,1)S(1)} %get-tuple-element.5.onehots), custom_call_target="tpu_custom_call" | custom-call | tf_op jit(solution)/shard_map/pallas_call | solution.py:365

commit v4 on v3

--- a/solution.py
+++ b/solution.py
@@ -8,10 +8,11 @@
 from jax.sharding import PartitionSpec as P
 
 BLOCK = 128
-COMPS = 16
+COMPS, VOLUME = 16, 14
+RING_STEPS = (-2, -1, 0)
 SHIFT = 0.1
 SYM = ((0, 0), (1, 1), (2, 2), (0, 1), (0, 2), (1, 2))
-DIRS = tuple((dx, dy) for dx in (-1, 0, 1) for dy in (-1, 0, 1) if (dx, dy) != (0, 0))
+DIRS = ((-1, -1), (-1, 1), (1, -1), (1, 1), (0, -1), (0, 1), (-1, 0), (1, 0))
 MESH = pl.DeviceIdType.MESH
 
 
@@ -130,10 +131,12 @@
             conditions.append(gy < n_gy - 1 if dy > 0 else gy > 0)
         return functools.reduce(jnp.logical_and, conditions)
 
+    fill_row = lax.broadcasted_iota(jnp.int32, (COMPS, BLOCK), 0)
+    far = 4096.0 + 8.0 * lax.broadcasted_iota(jnp.int32, (COMPS, BLOCK), 1).astype(F32)
     for rx in range(4):
         for ry in range(4):
             if rx in (0, 3) or ry in (0, 3):
-                region[rx, ry] = jnp.zeros((COMPS, BLOCK), F32)
+                region[rx, ry] = jnp.where(fill_row == 0, far + 4096.0 * (rx * 4 + ry), 0.0)
 
     barrier = pltpu.get_barrier_semaphore()
     for dx, dy in DIRS:
@@ -152,10 +155,11 @@
         lanes = pl.ds(block * BLOCK, BLOCK)
         packed[block, 0:3, :] = ref_ref[:, lanes]
         packed[block, 3:6, :] = disp_ref[:, lanes]
-        packed[block, 6:7, :] = vol_ref[:, lanes]
+        packed[block, 6:7, :] = vol_ref[:, lanes] * (1.5 / 8.0)
         packed[block, 7:13, :] = plastic_ref[:, lanes]
         packed[block, 13:14, :] = material_ref[:, lanes].astype(F32)
-        packed[block, 14:16, :] = jnp.zeros((2, BLOCK), F32)
+        packed[block, 14:15, :] = vol_ref[:, lanes]
+        packed[block, 15:16, :] = jnp.zeros((1, BLOCK), F32)
         near = jnp.floor(ref_ref[:, lanes] + 0.5)
         near = near - jnp.min(near, axis=1, keepdims=True)
         site = near[0:1] * 32.0 + near[1:2] * 8.0 + near[2:3]
@@ -207,6 +211,7 @@
     force_ref,
     plastic_out_ref,
     state,
+    pairs,
     rolled,
     weights,
     piolas,
@@ -225,64 +230,88 @@
             high = jnp.where(chunk == 2, turned[2], turned[3])
             value = jnp.where(chunk < 2, low, high)
             row = (rx * 4 + x + 4) % 16
-            state[pl.ds(row, COMPS, stride=16), :] = value
-
-    def piece(comp, part):
-        return state[pl.ds(comp * 16 + part * 8, 8), :]
+            state[pl.ds(row, COMPS, stride=24), :] = value
+            if row < 8:
+                state[pl.ds(row + 16, COMPS, stride=24), :] = value
+
+    def rows(comp, start):
+        return state[pl.ds(comp * 24 + start, 8), :]
+
+    lower = lax.broadcasted_iota(jnp.int32, (8, BLOCK), 0) < 4
+
+    def ring_rows(comp, step):
+        return jnp.where(lower, rows(comp, 6 + step), rows(comp, 12 + step))
+
+    twice = lax.broadcasted_iota(jnp.int32, (8, BLOCK), 0) % 4 < 2
+    for step in RING_STEPS:
+        for c in range(7):
+            pairs[step + 2, c] = ring_rows(c, step)
+
+    def doubled(value):
+        return jnp.where(twice, value, pltpu.roll(value, 2, 0))
 
     z_lane = lax.broadcasted_iota(jnp.int32, (8, BLOCK), 1) % 8
-    home = [[piece(c, part) for c in range(3)] for part in range(2)]
+    home = [[doubled(ring_rows(c, 0)) for c in range(3)], [rows(c, 8) for c in range(3)]]
+
+    def add_visit(acc, place, other, reach, shift, alone=True):
+        if shift:
+            other = [pltpu.roll(value, shift, 1) for value in other]
+        dX = [other[a] - place[a] for a in range(3)]
+        square = dX[0] * dX[0] + dX[1] * dX[1] + dX[2] * dX[2]
+        dist = square * lax.rsqrt(square if alone else jnp.maximum(square, 1e-20))
+        t = jnp.maximum(reach - dist, 0.0)
+        w = (other[6] * t) * (t * t)
+        g = [w * dX[a] for a in range(3)]
+        for s, (a, b) in enumerate(SYM):
+            acc[s] = acc[s] + g[a] * dX[b]
+        for a in range(3):
+            for b in range(3):
+                acc[6 + 3 * a + b] = acc[6 + 3 * a + b] + other[3 + a] * g[b]
+        for a in range(3):
+            acc[15 + a] = acc[15 + a] + g[a]
+        return g
 
     def moment_visit(slot, sy, sz, x_steps, sums):
         shift = -(8 * sy + sz) % 128
         inside = (z_lane + sz >= 0) & (z_lane + sz < 8)
         reach = jnp.where(inside, 2.0, -100.0)
         for c in range(7):
-            for part in range(2):
-                value = scaled[part] if c == 6 else piece(c, part)
-                if shift:
-                    value = pltpu.roll(value, shift, 1)
-                rolled[slot, pl.ds(c * 32 + part * 8, 8), :] = value
-                rolled[slot, pl.ds(c * 32 + part * 8 + 16, 8), :] = value
+            ring, inner = rows(c, 0), rows(c, 8)
+            if shift:
+                ring, inner = pltpu.roll(ring, shift, 1), pltpu.roll(inner, shift, 1)
+            rolled[slot, pl.ds(c * 24, 8), :] = ring
+            rolled[slot, pl.ds(c * 24 + 8, 8), :] = inner
+            rolled[slot, pl.ds(c * 24 + 16, 8), :] = ring
         for sx in x_steps:
             if (sx, sy, sz) == (0, 0, 0):
                 continue
-            for part in range(2):
-                base = 8 if part == 1 else 16
-                other = [rolled[slot, pl.ds(c * 32 + base + sx, 8), :] for c in range(7)]
-                dX = [other[a] - home[part][a] for a in range(3)]
-                square = dX[0] * dX[0] + dX[1] * dX[1] + dX[2] * dX[2]
-                dist = square * lax.rsqrt(jnp.maximum(square, 1e-20))
-                t = jnp.maximum(reach - dist, 0.0)
-                w = (other[6] * t) * (t * t)
-                g = [w * dX[a] for a in range(3)]
-                acc = sums[part]
-                for s, (a, b) in enumerate(SYM):
-                    acc[s] = acc[s] + g[a] * dX[b]
-                for a in range(3):
-                    for b in range(3):
-                        acc[6 + 3 * a + b] = acc[6 + 3 * a + b] + other[3 + a] * g[b]
-                for a in range(3):
-                    acc[15 + a] = acc[15 + a] + g[a]
-                if part == 1:
-                    for a in range(3):
-                        weights[slot, (sx + 2) * 3 + a] = g[a]
+            other = [rolled[slot, pl.ds(c * 24 + 8 + sx, 8), :] for c in range(7)]
+            g = add_visit(sums[1], home[1], other, reach, 0)
+            for a in range(3):
+                weights[slot, (sx + 2) * 3 + a] = g[a]
+        for step in RING_STEPS:
+            if step == 0 and 2 not in x_steps or step == -1 and 1 not in x_steps:
+                continue
+            limit = reach if step < 0 else jnp.where(twice, -100.0, reach)
+            add_visit(sums[0], home[0], [pairs[step + 2, c] for c in range(7)], limit, shift, shift != 0)
 
     zero = jnp.zeros((8, BLOCK), F32)
-    scaled = [piece(6, part) * (1.5 / 8.0) for part in range(2)]
     sums = [[zero] * 18 for _ in range(2)]
     for slot, (sy, sz, x_steps) in enumerate(OFFSETS):
         moment_visit(slot, sy, sz, x_steps, sums)
 
+    sums[0] = [value + pltpu.roll(value, 6, 0) for value in sums[0]]
     own_piola, own_plastic = None, None
-    for part in range(2):
-        acc = sums[part]
-        disp = [piece(3 + a, part) for a in range(3)]
-        strain_sum = [acc[6 + 3 * a + b] - disp[a] * acc[15 + b] for a in range(3) for b in range(3)]
-        plastic = [piece(7 + s, part) for s in range(6)]
-        piola, plastic_new = constitutive(acc[0:6], strain_sum, plastic, piece(13, part))
+    for part, acc in enumerate(sums):
+        local = [rows(c, 8) if part == 1 else ring_rows(c, 0) for c in range(COMPS)]
+        strain_sum = [acc[6 + 3 * a + b] - local[3 + a] * acc[15 + b] for a in range(3) for b in range(3)]
+        piola, plastic_new = constitutive(acc[0:6], strain_sum, local[7:13], local[13])
         for c in range(9):
-            piolas[c, pl.ds(part * 8, 8), :] = piola[c]
+            if part == 1:
+                piolas[c, 8:16, :] = piola[c]
+            else:
+                piolas[c, 6:8, :] = piola[c][0:2]
+                piolas[c, 0:2, :] = piola[c][4:6]
         if part == 1:
             own_piola, own_plastic = piola, plastic_new
     for s in range(6):
@@ -308,17 +337,17 @@
                     other = rolled_piolas[slot, pl.ds((3 * a + b) * 24 + 8 + sx, 8), :]
                     force[a] = force[a] + other * g[b]
 
-    volume = piece(6, 1)
+    volume = rows(VOLUME, 8)
     for a in range(3):
         results[pl.ds(a * 8, 8), :] = volume * force[a]
     for c in range(9, 16):
         results[pl.ds(c * 8, 8), :] = zero
 
     for bx in range(2):
-        rows = [results[pl.ds(bx * 4 + x, COMPS, stride=8), :] for x in range(4)]
+        lines = [results[pl.ds(bx * 4 + x, COMPS, stride=8), :] for x in range(4)]
         for by in range(2):
             block = bx * 2 + by
-            turned = [pltpu.roll(rows[x], 32 * (x - by - 1) % 128, 1) for x in range(4)]
+            turned = [pltpu.roll(lines[x], 32 * (x - by - 1) % 128, 1) for x in range(4)]
             low = jnp.where(chunk == 0, turned[0], turned[1])
             high = jnp.where(chunk == 2, turned[2], turned[3])
             value = exact_product(jnp.where(chunk < 2, low, high), onehots[block], 0)
@@ -371,8 +400,9 @@
             in_specs=[vmem] * 2,
             out_specs=(vmem, vmem),
             scratch_shapes=[
-                pltpu.VMEM((COMPS * 16, BLOCK), F32),
-                pltpu.VMEM((25, 7 * 32, BLOCK), F32),
+                pltpu.VMEM((COMPS * 24, BLOCK), F32),
+                pltpu.VMEM((3, 7, 8, BLOCK), F32),
+                pltpu.VMEM((25, 7 * 24, BLOCK), F32),
                 pltpu.VMEM((25, 15, 8, BLOCK), F32),
                 pltpu.VMEM((9, 16, BLOCK), F32),
                 pltpu.VMEM((25, 9 * 24, BLOCK), F32),

time: 13.1 us -> 12.6 us (0.962)
  Pallas kernels: 12.3 us -> 11.9 us
    pallas_call x1, Pallas kernels: 3.19 us -> 2.9 us  [on_device(): pl.pallas_call(stencil_kernel, out_shape=(jax.ShapeDtypeStruct((3, count)...]
    pallas_call x1, Pallas kernels: 9.12 us -> 8.95 us  [on_device(): pl.pallas_call(functools.partial(exchange_kernel, n_gx, n_gy), out_shape=...]
where the time goes in v4:
time: 12.6 us; the launch traced here: 12.5 us
  Pallas kernels  11.9 us (94%)
  between operations  0.64 us (5%)
    pallas_call x1, Pallas kernels, on_device(): pl.pallas_call(functools.partial(exchange_kernel, n_gx, n_gy), out_shape=...  8.95 us
    pallas_call x1, Pallas kernels, on_device(): pl.pallas_call(stencil_kernel, out_shape=(jax.ShapeDtypeStruct((3, count)...  2.9 us

profile of v4, /device:TPU:103, one launch (start us, length us, event | category | flops | bytes accessed | tf_op | source)
XLA Modules:
  0.0 12.5 jit_solution(18280726762570304475)
XLA Ops:
  0.6 8.9 %shard_map.68 = (f32[4,4,16,128]{3,2,1,0:T(8,128)S(1)}, bf16[4,128,128]{2,1,0:T(8,128)(2,1)S(1)}) custom-call(f32[3,512]{1,0:T(4,128)} %ref_hbm.1, f32[3,512]{1,0:T(4,128)} %disp_hbm.1, f32[1,512]{1,0:T(1,128)} %bitcast.2, f32[6,512]{1,0:T(8,128)} %plastic_hbm.1, s32[1,512]{1,0:T(1,128)} %bitcast.3), custom_call_target="tpu_custom_call" | custom-call | tf_op jit(solution)/shard_map/pallas_call | solution.py:371
  9.6 2.9 %shard_map.69 = (f32[3,512]{1,0:T(4,128)}, f32[6,512]{1,0:T(8,128)}) custom-call(f32[4,4,16,128]{3,2,1,0:T(8,128)S(1)} %get-tuple-element.4.region, bf16[4,128,128]{2,1,0:T(8,128)(2,1)S(1)} %get-tuple-element.5.onehots), custom_call_target="tpu_custom_call" | custom-call | tf_op jit(solution)/shard_map/pallas_call | solution.py:394

commit v5 on v4

--- a/solution.py
+++ b/solution.py
@@ -10,9 +10,10 @@
 BLOCK = 128
 COMPS, VOLUME = 16, 14
 RING_STEPS = (-2, -1, 0)
+BEYOND = {2: (0,), 3: (1, 2, 3), 12: (4, 5, 6), 13: (7,)}
 SHIFT = 0.1
 SYM = ((0, 0), (1, 1), (2, 2), (0, 1), (0, 2), (1, 2))
-DIRS = ((-1, -1), (-1, 1), (1, -1), (1, 1), (0, -1), (0, 1), (-1, 0), (1, 0))
+DIRS = ((0, -1), (0, 1), (-1, -1), (-1, 1), (1, -1), (1, 1), (-1, 0), (1, 0))
 MESH = pl.DeviceIdType.MESH
 
 
@@ -86,6 +87,46 @@
     return piola, plastic_new
 
 
+def reach_of(sz):
+    z_lane = lax.broadcasted_iota(jnp.int32, (8, BLOCK), 1) % 8
+    return jnp.where((z_lane + sz >= 0) & (z_lane + sz < 8), 2.0, -100.0)
+
+
+def lane_turn(sy, sz):
+    return -(8 * sy + sz) % 128
+
+
+def turn(values, shift):
+    return [pltpu.roll(value, shift, 1) for value in values] if shift else list(values)
+
+
+def rows_of_blocks(blocks, x):
+    chunk = lax.broadcasted_iota(jnp.int32, (COMPS, BLOCK), 1) // 32
+    turned = [
+        pltpu.roll(blocks[ry], 32 * (ry - x) % 128, 1) if ry != x else blocks[ry] for ry in range(4)
+    ]
+    low = jnp.where(chunk == 0, turned[0], turned[1])
+    high = jnp.where(chunk == 2, turned[2], turned[3])
+    return jnp.where(chunk < 2, low, high)
+
+
+def add_visit(acc, place, other, reach, alone):
+    dX = [other[a] - place[a] for a in range(3)]
+    square = dX[0] * dX[0] + dX[1] * dX[1] + dX[2] * dX[2]
+    dist = square * lax.rsqrt(square if alone else jnp.maximum(square, 1e-20))
+    t = jnp.maximum(reach - dist, 0.0)
+    w = (other[6] * t) * (t * t)
+    g = [w * dX[a] for a in range(3)]
+    for s, (a, b) in enumerate(SYM):
+        acc[s] = acc[s] + g[a] * dX[b]
+    for a in range(3):
+        for b in range(3):
+            acc[6 + 3 * a + b] = acc[6 + 3 * a + b] + other[3 + a] * g[b]
+    for a in range(3):
+        acc[15 + a] = acc[15 + a] + g[a]
+    return g
+
+
 def exchange_kernel(
     n_gx,
     n_gy,
@@ -96,12 +137,16 @@
     material_hbm,
     region,
     onehots,
+    core,
+    core_sums,
+    weights,
     ref_ref,
     disp_ref,
     vol_ref,
     plastic_ref,
     material_ref,
     packed,
+    rolled,
     load_sem,
     send_sem,
     recv_sem,
@@ -192,12 +237,38 @@
         def _():
             copy_to(number).start()
 
-    for number, (dx, dy) in enumerate(DIRS):
-
-        @pl.when(present(-dx, -dy))
-        def _():
-            copy_to(number).wait_recv()
-
+    def receive(chosen):
+        for number, (dx, dy) in enumerate(DIRS):
+            if chosen(dx):
+                pl.when(present(-dx, -dy))(lambda number=number: copy_to(number).wait_recv())
+
+    receive(lambda dx: dx == 0)
+    for rx in (1, 2):
+        blocks = [region[rx, ry] for ry in range(4)]
+        for x in range(4):
+            core[pl.ds(rx * 4 + x - 4, COMPS, stride=8), :] = rows_of_blocks(blocks, x)
+    row = lax.broadcasted_iota(jnp.int32, (8, BLOCK), 0)
+    zero = jnp.zeros((8, BLOCK), F32)
+    home = [core[pl.ds(c * 8, 8), :] for c in range(7)]
+    sums = [zero] * 18
+    for slot, (sy, sz, x_steps) in enumerate(OFFSETS):
+        rolled[slot, 0:8, :] = zero
+        rolled[slot, 64:72, :] = zero
+        for c, value in enumerate(turn(home, lane_turn(sy, sz))):
+            rolled[slot, pl.ds(8 + c * 8, 8), :] = value
+        reach = reach_of(sz)
+        for sx in x_steps:
+            if (sx, sy, sz) == (0, 0, 0):
+                continue
+            other = [rolled[slot, pl.ds(8 + c * 8 + sx, 8), :] for c in range(7)]
+            limit = jnp.where((row + sx >= 0) & (row + sx < 8), reach, -100.0) if sx else reach
+            g = add_visit(sums, home, other, limit, sx == 0)
+            for a in range(3):
+                weights[slot, (sx + 2) * 3 + a] = g[a]
+    for s in range(18):
+        core_sums[s] = sums[s]
+
+    receive(lambda dx: dx != 0)
     for number, (dx, dy) in enumerate(DIRS):
 
         @pl.when(present(dx, dy))
@@ -208,31 +279,29 @@
 def stencil_kernel(
     region,
     onehots,
+    core,
+    core_sums,
+    weights,
     force_ref,
     plastic_out_ref,
     state,
     pairs,
-    rolled,
-    weights,
-    piolas,
+    beyond,
+    beyond_weights,
     rolled_piolas,
     results,
 ):
-    chunk = lax.broadcasted_iota(jnp.int32, (COMPS, BLOCK), 1) // 32
-    for rx in range(4):
+    for c in range(COMPS):
+        state[pl.ds(c * 24 + 8, 8), :] = core[pl.ds(c * 8, 8), :]
+    for rx in (0, 3):
         blocks = [region[rx, ry] for ry in range(4)]
         for x in range(4):
-            turned = [
-                pltpu.roll(blocks[ry], 32 * (ry - x) % 128, 1) if ry != x else blocks[ry]
-                for ry in range(4)
-            ]
-            low = jnp.where(chunk == 0, turned[0], turned[1])
-            high = jnp.where(chunk == 2, turned[2], turned[3])
-            value = jnp.where(chunk < 2, low, high)
-            row = (rx * 4 + x + 4) % 16
-            state[pl.ds(row, COMPS, stride=24), :] = value
-            if row < 8:
-                state[pl.ds(row + 16, COMPS, stride=24), :] = value
+            value = rows_of_blocks(blocks, x)
+            place = (rx * 4 + x + 4) % 16
+            state[pl.ds(place, COMPS, stride=24), :] = value
+            state[pl.ds(place + 16, COMPS, stride=24), :] = value
+            for target in BEYOND.get(rx * 4 + x, ()):
+                beyond[pl.ds(target, COMPS, stride=8), :] = value
 
     def rows(comp, start):
         return state[pl.ds(comp * 24 + start, 8), :]
@@ -250,92 +319,74 @@
     def doubled(value):
         return jnp.where(twice, value, pltpu.roll(value, 2, 0))
 
-    z_lane = lax.broadcasted_iota(jnp.int32, (8, BLOCK), 1) % 8
-    home = [[doubled(ring_rows(c, 0)) for c in range(3)], [rows(c, 8) for c in range(3)]]
-
-    def add_visit(acc, place, other, reach, shift, alone=True):
-        if shift:
-            other = [pltpu.roll(value, shift, 1) for value in other]
-        dX = [other[a] - place[a] for a in range(3)]
-        square = dX[0] * dX[0] + dX[1] * dX[1] + dX[2] * dX[2]
-        dist = square * lax.rsqrt(square if alone else jnp.maximum(square, 1e-20))
-        t = jnp.maximum(reach - dist, 0.0)
-        w = (other[6] * t) * (t * t)
-        g = [w * dX[a] for a in range(3)]
-        for s, (a, b) in enumerate(SYM):
-            acc[s] = acc[s] + g[a] * dX[b]
-        for a in range(3):
-            for b in range(3):
-                acc[6 + 3 * a + b] = acc[6 + 3 * a + b] + other[3 + a] * g[b]
-        for a in range(3):
-            acc[15 + a] = acc[15 + a] + g[a]
-        return g
-
-    def moment_visit(slot, sy, sz, x_steps, sums):
-        shift = -(8 * sy + sz) % 128
-        inside = (z_lane + sz >= 0) & (z_lane + sz < 8)
-        reach = jnp.where(inside, 2.0, -100.0)
-        for c in range(7):
-            ring, inner = rows(c, 0), rows(c, 8)
-            if shift:
-                ring, inner = pltpu.roll(ring, shift, 1), pltpu.roll(inner, shift, 1)
-            rolled[slot, pl.ds(c * 24, 8), :] = ring
-            rolled[slot, pl.ds(c * 24 + 8, 8), :] = inner
-            rolled[slot, pl.ds(c * 24 + 16, 8), :] = ring
-        for sx in x_steps:
-            if (sx, sy, sz) == (0, 0, 0):
-                continue
-            other = [rolled[slot, pl.ds(c * 24 + 8 + sx, 8), :] for c in range(7)]
-            g = add_visit(sums[1], home[1], other, reach, 0)
-            for a in range(3):
-                weights[slot, (sx + 2) * 3 + a] = g[a]
+    row = lax.broadcasted_iota(jnp.int32, (8, BLOCK), 0)
+    used = (row < 3) | (row > 4)
+
+    def facing(value):
+        return jnp.where(row == 2, pltpu.roll(value, 2, 0), jnp.where(row == 5, pltpu.roll(value, 6, 0), value))
+
+    def gathered(value):
+        paired = jnp.where(row == 0, pltpu.roll(value, 6, 0), jnp.where(row == 7, pltpu.roll(value, 2, 0), 0.0))
+        return jnp.where((row < 2) | (row > 5), value + paired, 0.0)
+
+    home = [doubled(ring_rows(c, 0)) for c in range(3)]
+    edge = [facing(rows(c, 8)) for c in range(3)]
+    sources = [beyond[pl.ds(c * 8, 8), :] for c in range(7)]
+    zero = jnp.zeros((8, BLOCK), F32)
+    ring_sums, edge_sums = [zero] * 18, [zero] * 18
+    for slot, (sy, sz, x_steps) in enumerate(OFFSETS):
+        shift = lane_turn(sy, sz)
+        reach = reach_of(sz)
         for step in RING_STEPS:
             if step == 0 and 2 not in x_steps or step == -1 and 1 not in x_steps:
                 continue
             limit = reach if step < 0 else jnp.where(twice, -100.0, reach)
-            add_visit(sums[0], home[0], [pairs[step + 2, c] for c in range(7)], limit, shift, shift != 0)
-
-    zero = jnp.zeros((8, BLOCK), F32)
-    sums = [[zero] * 18 for _ in range(2)]
-    for slot, (sy, sz, x_steps) in enumerate(OFFSETS):
-        moment_visit(slot, sy, sz, x_steps, sums)
-
-    sums[0] = [value + pltpu.roll(value, 6, 0) for value in sums[0]]
-    own_piola, own_plastic = None, None
-    for part, acc in enumerate(sums):
-        local = [rows(c, 8) if part == 1 else ring_rows(c, 0) for c in range(COMPS)]
+            other = turn([pairs[step + 2, c] for c in range(7)], shift)
+            add_visit(ring_sums, home, other, limit, shift != 0)
+        if 1 in x_steps:
+            limit = jnp.where(used, reach, -100.0)
+            g = add_visit(edge_sums, edge, turn(sources, shift), limit, True)
+            for a in range(3):
+                beyond_weights[slot, a] = g[a]
+
+    ring_sums = [value + pltpu.roll(value, 6, 0) for value in ring_sums]
+    own_sums = [core_sums[s] + gathered(edge_sums[s]) for s in range(18)]
+
+    def stresses(acc, local):
         strain_sum = [acc[6 + 3 * a + b] - local[3 + a] * acc[15 + b] for a in range(3) for b in range(3)]
-        piola, plastic_new = constitutive(acc[0:6], strain_sum, local[7:13], local[13])
-        for c in range(9):
-            if part == 1:
-                piolas[c, 8:16, :] = piola[c]
-            else:
-                piolas[c, 6:8, :] = piola[c][0:2]
-                piolas[c, 0:2, :] = piola[c][4:6]
-        if part == 1:
-            own_piola, own_plastic = piola, plastic_new
+        return constitutive(acc[0:6], strain_sum, local[7:13], local[13])
+
+    own_piola, own_plastic = stresses(own_sums, [rows(c, 8) for c in range(COMPS)])
+    ring_piola, _ = stresses(ring_sums, [ring_rows(c, 0) for c in range(COMPS)])
+    ring_piola = [
+        jnp.where(row < 2, value, jnp.where(row < 6, pltpu.roll(value, 1, 0), pltpu.roll(value, 2, 0)))
+        for value in ring_piola
+    ]
     for s in range(6):
         results[pl.ds((3 + s) * 8, 8), :] = own_plastic[s]
-    lean = sums[1][15:18]
+    lean = own_sums[15:18]
     force = [sum(own_piola[3 * a + b] * lean[b] for b in range(3)) for a in range(3)]
-
+    edge_force = [zero] * 3
     for slot, (sy, sz, x_steps) in enumerate(OFFSETS):
-        shift = -(8 * sy + sz) % 128
-        for c in range(9):
-            ring, inner = piolas[c, 0:8, :], piolas[c, 8:16, :]
-            if shift:
-                ring, inner = pltpu.roll(ring, shift, 1), pltpu.roll(inner, shift, 1)
-            rolled_piolas[slot, pl.ds(c * 24, 8), :] = ring
-            rolled_piolas[slot, pl.ds(c * 24 + 8, 8), :] = inner
-            rolled_piolas[slot, pl.ds(c * 24 + 16, 8), :] = ring
+        shift = lane_turn(sy, sz)
+        rolled_piolas[slot, 0:8, :] = zero
+        rolled_piolas[slot, 80:88, :] = zero
+        for c, value in enumerate(turn(own_piola, shift)):
+            rolled_piolas[slot, pl.ds(8 + c * 8, 8), :] = value
         for sx in x_steps:
             if (sx, sy, sz) == (0, 0, 0):
                 continue
             g = [weights[slot, (sx + 2) * 3 + a] for a in range(3)]
             for a in range(3):
                 for b in range(3):
-                    other = rolled_piolas[slot, pl.ds((3 * a + b) * 24 + 8 + sx, 8), :]
+                    other = rolled_piolas[slot, pl.ds(8 + (3 * a + b) * 8 + sx, 8), :]
                     force[a] = force[a] + other * g[b]
+        if 1 in x_steps:
+            other = turn(ring_piola, shift)
+            for a in range(3):
+                for b in range(3):
+                    edge_force[a] = edge_force[a] + other[3 * a + b] * beyond_weights[slot, b]
+    force = [force[a] + gathered(edge_force[a]) for a in range(3)]
 
     volume = rows(VOLUME, 8)
     for a in range(3):
@@ -343,6 +394,7 @@
     for c in range(9, 16):
         results[pl.ds(c * 8, 8), :] = zero
 
+    chunk = lax.broadcasted_iota(jnp.int32, (COMPS, BLOCK), 1) // 32
     for bx in range(2):
         lines = [results[pl.ds(bx * 4 + x, COMPS, stride=8), :] for x in range(4)]
         for by in range(2):
@@ -368,14 +420,17 @@
                 ref_pos, disp, volume.reshape(1, count), plastic, material.reshape(1, count)
             )
         ]
-        region, onehots = pl.pallas_call(
+        shared = pl.pallas_call(
             functools.partial(exchange_kernel, n_gx, n_gy),
             out_shape=(
                 jax.ShapeDtypeStruct((4, 4, COMPS, BLOCK), F32),
                 jax.ShapeDtypeStruct((4, BLOCK, BLOCK), jnp.bfloat16),
+                jax.ShapeDtypeStruct((COMPS * 8, BLOCK), F32),
+                jax.ShapeDtypeStruct((18, 8, BLOCK), F32),
+                jax.ShapeDtypeStruct((25, 15, 8, BLOCK), F32),
             ),
             in_specs=[pl.BlockSpec(memory_space=pltpu.HBM)] * 5,
-            out_specs=(vmem, vmem),
+            out_specs=(vmem,) * 5,
             scratch_shapes=[
                 pltpu.VMEM((3, count), F32),
                 pltpu.VMEM((3, count), F32),
@@ -383,12 +438,13 @@
                 pltpu.VMEM((6, count), F32),
                 pltpu.VMEM((1, count), jnp.int32),
                 pltpu.VMEM((4, COMPS, BLOCK), F32),
+                pltpu.VMEM((25, 72, BLOCK), F32),
                 pltpu.SemaphoreType.DMA((5,)),
                 pltpu.SemaphoreType.DMA((8,)),
                 pltpu.SemaphoreType.DMA((8,)),
             ],
             compiler_params=pltpu.CompilerParams(
-                collective_id=0, has_side_effects=True, vmem_limit_bytes=4 << 20
+                collective_id=0, has_side_effects=True, vmem_limit_bytes=8 << 20
             ),
         )(*inputs)
         return pl.pallas_call(
@@ -397,19 +453,18 @@
                 jax.ShapeDtypeStruct((3, count), F32),
                 jax.ShapeDtypeStruct((6, count), F32),
             ),
-            in_specs=[vmem] * 2,
+            in_specs=[vmem] * 5,
             out_specs=(vmem, vmem),
             scratch_shapes=[
                 pltpu.VMEM((COMPS * 24, BLOCK), F32),
                 pltpu.VMEM((3, 7, 8, BLOCK), F32),
-                pltpu.VMEM((25, 7 * 24, BLOCK), F32),
-                pltpu.VMEM((25, 15, 8, BLOCK), F32),
-                pltpu.VMEM((9, 16, BLOCK), F32),
-                pltpu.VMEM((25, 9 * 24, BLOCK), F32),
+                pltpu.VMEM((COMPS * 8, BLOCK), F32),
+                pltpu.VMEM((25, 3, 8, BLOCK), F32),
+                pltpu.VMEM((25, 88, BLOCK), F32),
                 pltpu.VMEM((COMPS * 8, BLOCK), F32),
             ],
             compiler_params=pltpu.CompilerParams(vmem_limit_bytes=16 << 20),
-        )(region, onehots)
+        )(*shared)
 
     in_specs = (
         P(None, ("gx", "gy")),

time: 12.6 us -> 12.2 us (0.968)
  Pallas kernels: 11.9 us -> 11.4 us
    pallas_call x1, Pallas kernels: 2.9 us -> 2.33 us  [on_device(): pl.pallas_call(stencil_kernel, out_shape=(jax.ShapeDtypeStruct((3, count)...]
    pallas_call x1, Pallas kernels: 8.95 us -> 9.1 us  [on_device(): pl.pallas_call(functools.partial(exchange_kernel, n_gx, n_gy), out_shape=...]
where the time goes in v5:
time: 12.2 us; the launch traced here: 12.1 us
  Pallas kernels  11.4 us (93%)
  between operations  0.64 us (5%)
    pallas_call x1, Pallas kernels, on_device(): pl.pallas_call(functools.partial(exchange_kernel, n_gx, n_gy), out_shape=...  9.1 us
    pallas_call x1, Pallas kernels, on_device(): pl.pallas_call(stencil_kernel, out_shape=(jax.ShapeDtypeStruct((3, count)...  2.33 us

profile of v5, /device:TPU:103, one launch (start us, length us, event | category | flops | bytes accessed | tf_op | source)
XLA Modules:
  0.0 12.1 jit_solution(9255004179137004853)
XLA Ops:
  0.6 9.1 %shard_map.68 = (f32[4,4,16,128]{3,2,1,0:T(8,128)S(1)}, bf16[4,128,128]{2,1,0:T(8,128)(2,1)S(1)}, f32[128,128]{1,0:T(8,128)S(1)}, f32[18,8,128]{2,1,0:T(8,128)S(1)}, f32[25,15,8,128]{3,2,1,0:T(8,128)S(1)}) custom-call(f32[3,512]{1,0:T(4,128)} %ref_hbm.1, f32[3,512]{1,0:T(4,128)} %disp_hbm.1, f32[1,512]{1,0:T(1,128)} %bitcast.2, f32[6,512]{1,0:T(8,128)} %plastic_hbm.1, ...), custom_call_target="tpu_custom_call" | custom-call | tf_op jit(solution)/shard_map/pallas_call | solution.py:423
  9.7 2.3 %shard_map.69 = (f32[3,512]{1,0:T(4,128)}, f32[6,512]{1,0:T(8,128)}) custom-call(f32[4,4,16,128]{3,2,1,0:T(8,128)S(1)} %get-tuple-element.7.region, bf16[4,128,128]{2,1,0:T(8,128)(2,1)S(1)} %get-tuple-element.8.onehots, f32[128,128]{1,0:T(8,128)S(1)} %get-tuple-element.9.core, f32[18,8,128]{2,1,0:T(8,128)S(1)} %get-tuple-element.10.core_sums, ...), custom_call_target="tpu_custom_call" | custom-call | tf_op jit(solution)/shard_map/pallas_call | solution.py:450

commit v6 on v5

--- a/solution.py
+++ b/solution.py
@@ -13,7 +13,7 @@
 BEYOND = {2: (0,), 3: (1, 2, 3), 12: (4, 5, 6), 13: (7,)}
 SHIFT = 0.1
 SYM = ((0, 0), (1, 1), (2, 2), (0, 1), (0, 2), (1, 2))
-DIRS = ((0, -1), (0, 1), (-1, -1), (-1, 1), (1, -1), (1, 1), (-1, 0), (1, 0))
+DIRS = ((0, -1), (0, 1), (-1, -1), (-1, 1), (-1, 0), (1, -1), (1, 1), (1, 0))
 MESH = pl.DeviceIdType.MESH
 
 
@@ -146,6 +146,7 @@
     plastic_ref,
     material_ref,
     packed,
+    inner,
     rolled,
     load_sem,
     send_sem,
@@ -242,18 +243,27 @@
             if chosen(dx):
                 pl.when(present(-dx, -dy))(lambda number=number: copy_to(number).wait_recv())
 
+    zero = jnp.zeros((8, BLOCK), F32)
+    for slot in range(len(OFFSETS)):
+        rolled[slot, 0:8, :] = zero
+        rolled[slot, 64:72, :] = zero
+    chunk = lax.broadcasted_iota(jnp.int32, (COMPS, BLOCK), 1) // 32
+    for rx in (1, 2):
+        blocks = [region[rx, 1], region[rx, 2]]
+        for x in range(4):
+            first, second = (pltpu.roll(blocks[k], 32 * (k + 1 - x) % 128, 1) for k in range(2))
+            inner[rx * 4 + x - 4] = jnp.where(chunk == 1, first, second)
     receive(lambda dx: dx == 0)
     for rx in (1, 2):
-        blocks = [region[rx, ry] for ry in range(4)]
+        blocks = [region[rx, 0], region[rx, 3]]
         for x in range(4):
-            core[pl.ds(rx * 4 + x - 4, COMPS, stride=8), :] = rows_of_blocks(blocks, x)
+            first, last = (pltpu.roll(blocks[k], 32 * (3 * k - x) % 128, 1) for k in range(2))
+            value = jnp.where(chunk == 0, first, jnp.where(chunk == 3, last, inner[rx * 4 + x - 4]))
+            core[pl.ds(rx * 4 + x - 4, COMPS, stride=8), :] = value
     row = lax.broadcasted_iota(jnp.int32, (8, BLOCK), 0)
-    zero = jnp.zeros((8, BLOCK), F32)
     home = [core[pl.ds(c * 8, 8), :] for c in range(7)]
     sums = [zero] * 18
     for slot, (sy, sz, x_steps) in enumerate(OFFSETS):
-        rolled[slot, 0:8, :] = zero
-        rolled[slot, 64:72, :] = zero
         for c, value in enumerate(turn(home, lane_turn(sy, sz))):
             rolled[slot, pl.ds(8 + c * 8, 8), :] = value
         reach = reach_of(sz)
@@ -438,6 +448,7 @@
                 pltpu.VMEM((6, count), F32),
                 pltpu.VMEM((1, count), jnp.int32),
                 pltpu.VMEM((4, COMPS, BLOCK), F32),
+                pltpu.VMEM((8, COMPS, BLOCK), F32),
                 pltpu.VMEM((25, 72, BLOCK), F32),
                 pltpu.SemaphoreType.DMA((5,)),
                 pltpu.SemaphoreType.DMA((8,)),

time: 12.2 us -> 12.2 us (level)
  no operation moved by 1% of the time
where the time goes in v6:
time: 12.2 us; the launch traced here: 12 us
  Pallas kernels  11.4 us (93%)
  between operations  0.64 us (5%)
    pallas_call x1, Pallas kernels, on_device(): pl.pallas_call(functools.partial(exchange_kernel, n_gx, n_gy), out_shape=...  9.07 us
    pallas_call x1, Pallas kernels, on_device(): pl.pallas_call(stencil_kernel, out_shape=(jax.ShapeDtypeStruct((3, count)...  2.33 us

profile of v6, /device:TPU:103, one launch (start us, length us, event | category | flops | bytes accessed | tf_op | source)
XLA Modules:
  0.0 12.0 jit_solution(14199135105424385636)
XLA Ops:
  0.6 9.1 %shard_map.68 = (f32[4,4,16,128]{3,2,1,0:T(8,128)S(1)}, bf16[4,128,128]{2,1,0:T(8,128)(2,1)S(1)}, f32[128,128]{1,0:T(8,128)S(1)}, f32[18,8,128]{2,1,0:T(8,128)S(1)}, f32[25,15,8,128]{3,2,1,0:T(8,128)S(1)}) custom-call(f32[3,512]{1,0:T(4,128)} %ref_hbm.1, f32[3,512]{1,0:T(4,128)} %disp_hbm.1, f32[1,512]{1,0:T(1,128)} %bitcast.2, f32[6,512]{1,0:T(8,128)} %plastic_hbm.1, ...), custom_call_target="tpu_custom_call" | custom-call | tf_op jit(solution)/shard_map/pallas_call | solution.py:433
  9.7 2.3 %shard_map.69 = (f32[3,512]{1,0:T(4,128)}, f32[6,512]{1,0:T(8,128)}) custom-call(f32[4,4,16,128]{3,2,1,0:T(8,128)S(1)} %get-tuple-element.7.region, bf16[4,128,128]{2,1,0:T(8,128)(2,1)S(1)} %get-tuple-element.8.onehots, f32[128,128]{1,0:T(8,128)S(1)} %get-tuple-element.9.core, f32[18,8,128]{2,1,0:T(8,128)S(1)} %get-tuple-element.10.core_sums, ...), custom_call_target="tpu_custom_call" | custom-call | tf_op jit(solution)/shard_map/pallas_call | solution.py:461
